TPU v7x, 256 devices: a whole 4x4x8 slice. The times are simulated.
256 devices in a mesh: ctx: 64 (over z, x, core), head: 4 (over y).
Axes of the slice: x: 4, y: 4, z: 8, core: 2. Of those that a mesh axis runs over, the one named last changes fastest.
Arguments:
- inputs: bfloat16 [12288, 2048], P('ctx'), may hold values from -6 to 6
- projection: bfloat16 [3, 2048, 1024], P(None, None, 'head'), may hold values from -0.125 to 0.125
- conv_weight: float32 [3, 4, 1024], P(None, None, 'head'), may hold values from -3 to 3
- gate_code: int32 [8, 12288], P('head', 'ctx'), may hold values from 0 to 1023
- beta_code: int32 [8, 12288], P('head', 'ctx'), may hold values from 0 to 1023
- grad_out: bfloat16 [12288, 1024], P('ctx', 'head'), may hold values from -6 to 6
Outputs:
- input_grad: bfloat16 [12288, 2048], P(('ctx', 'head'))
- kernel_grad: float32 [3, 4, 1024], P(None, None, 'head')
All inputs are finite; a program needn't handle non-finite values.
Results may differ from a plain program's by a relative error of at most 0.0068.
The roundings to bfloat16 on the way count: a program that leaves them out, or rounds other values in their place, can miss the bound.
Values may be sent and summed in bfloat16 or wider, within the bound.
No kernel may reach another device: no remote copies, remote signals or barrier semaphores. Data moves between devices by JAX's collectives and lax.ppermute only.
A program may use at most 64 MiB of HBM per device.

v0:
```python
import jax
import jax.numpy as jnp
from jax import lax
from jax.sharding import PartitionSpec as P

DK = 128
KW = 4
GROUP = 64
HIGHEST_PRECISION = lax.Precision.HIGHEST


def from_behind(block, axis, distance):
    devices = range(lax.axis_size(axis))
    route = [(i - distance, i) for i in devices if i - distance in devices]
    return lax.ppermute(block, axis, route)


def normalize(matrix):
    return matrix * lax.rsqrt(jnp.sum(matrix * matrix, -1, keepdims=True) + 1e-06)


def features(extended, weights):
    length = extended.shape[1] - (KW - 1)
    convolved = weights[:, 0:1, :] * extended[:, 0:length, :]
    for offset in range(1, KW):
        convolved = (
            convolved
            + weights[:, offset : offset + 1, :] * extended[:, offset : offset + length, :]
        )
    activated = jax.nn.silu(convolved)
    head_count = activated.shape[2] // DK
    activated = activated.reshape(3, length, head_count, DK).transpose(0, 2, 1, 3)
    queries = normalize(activated[0]) * DK ** (-0.5)
    norm_keys = normalize(activated[1])
    return (queries, norm_keys, activated[2])


def block_step(carried, pieces):
    queries, norm_keys, value_rows, log_gate, beta_rate = pieces
    cumulative = jnp.cumsum(log_gate, axis=-1)
    decay_now = jnp.exp(cumulative)
    between = cumulative[:, :, None] - cumulative[:, None, :]
    position = jnp.arange(log_gate.shape[-1])
    strict = position[:, None] > position[None, :]
    inclusive = position[:, None] >= position[None, :]
    key_gram = jnp.einsum("htd,hsd->hts", norm_keys, norm_keys, precision=HIGHEST_PRECISION)
    lower_part = jnp.where(strict, jnp.exp(between), 0.0) * key_gram * beta_rate[:, :, None]
    recalled = jnp.einsum("htd,hvd->htv", norm_keys, carried, precision=HIGHEST_PRECISION)
    target = beta_rate[:, :, None] * (value_rows - decay_now[:, :, None] * recalled)
    pseudo = jax.scipy.linalg.solve_triangular(lower_part, target, lower=True, unit_diagonal=True)
    scores = jnp.einsum(
        "htd,hsd->hts", queries, norm_keys, precision=HIGHEST_PRECISION
    ) * jnp.where(inclusive, jnp.exp(between), 0.0)
    outputs = decay_now[:, :, None] * jnp.einsum(
        "htd,hvd->htv", queries, carried, precision=HIGHEST_PRECISION
    )
    outputs = outputs + jnp.einsum("hts,hsv->htv", scores, pseudo, precision=HIGHEST_PRECISION)
    group_total = cumulative[:, -1]
    remaining = jnp.exp(group_total[:, None] - cumulative)
    new_state = jnp.exp(group_total)[:, None, None] * carried
    new_state = new_state + jnp.einsum(
        "hsv,hsd->hvd", pseudo, remaining[:, :, None] * norm_keys, precision=HIGHEST_PRECISION
    )
    return (new_state, outputs)


def run_blocks(queries, norm_keys, value_rows, log_gate, beta_rate, carried):
    head_count = queries.shape[0]
    length = queries.shape[1]
    blocks = length // GROUP

    def to_blocks(tensor):
        return jnp.moveaxis(
            tensor.reshape((tensor.shape[0], blocks, GROUP) + tensor.shape[2:]), 1, 0
        )

    final_state, outputs = lax.scan(
        block_step,
        carried,
        (
            to_blocks(queries),
            to_blocks(norm_keys),
            to_blocks(value_rows),
            to_blocks(log_gate),
            to_blocks(beta_rate),
        ),
    )
    outputs = jnp.moveaxis(outputs, 0, 1).reshape(head_count, length, DK)
    return (outputs, final_state)


def chain_product(left_side, right_side):
    return jnp.einsum("hij,hjk->hik", left_side, right_side, precision=HIGHEST_PRECISION)


def on_device(inputs, projection, conv_weight, gate_code, beta_code, grad_out):
    length = inputs.shape[0]
    head_count = gate_code.shape[0]
    projected = jnp.stack(
        [
            jnp.dot(inputs, projection[member], preferred_element_type=jnp.float32)
            for member in range(3)
        ]
    ).astype(jnp.bfloat16)
    tail_rows = projected[:, length - (KW - 1) :, :]
    earlier_rows = from_behind(tail_rows, "ctx", 1)
    extended = jnp.concatenate([earlier_rows, projected], 1).astype(jnp.float32)
    log_gate = jnp.log(1.0 - 0.001 * gate_code.astype(jnp.float32) / 1023.0)
    beta_rate = beta_code.astype(jnp.float32) / 1023.0
    (queries, norm_keys, value_rows), feature_pull = jax.vjp(features, extended, conv_weight)
    identity = jnp.broadcast_to(jnp.eye(DK, dtype=jnp.float32), (head_count, DK, DK))
    zero_state = jnp.zeros((head_count, DK, DK), jnp.float32)
    paired = run_blocks(
        jnp.concatenate([queries, queries], 0),
        jnp.concatenate([norm_keys, norm_keys], 0),
        jnp.concatenate([value_rows, jnp.zeros_like(value_rows)], 0),
        jnp.concatenate([log_gate, log_gate], 0),
        jnp.concatenate([beta_rate, beta_rate], 0),
        jnp.concatenate([zero_state, identity], 0),
    )[1]
    local_state = paired[:head_count]
    transition = paired[head_count:]

    def advance(rounds, carried):
        return from_behind(chain_product(carried, transition) + local_state, "ctx", 1)

    entering = lax.fori_loop(0, lax.axis_size("ctx") - 1, advance, zero_state)

    def core(query_part, key_part, value_part, start_state):
        return run_blocks(query_part, key_part, value_part, log_gate, beta_rate, start_state)

    (outputs, leaving), core_pull = jax.vjp(core, queries, norm_keys, value_rows, entering)
    cotangent = grad_out.astype(jnp.float32).reshape(length, head_count, DK).transpose(1, 0, 2)
    direct_grads = core_pull((cotangent, zero_state))
    local_adjoint = direct_grads[3]
    flipped = jnp.swapaxes(transition, 1, 2)

    def retreat(rounds, carried):
        return from_behind(chain_product(carried, flipped) + local_adjoint, "ctx", -1)

    arriving = lax.fori_loop(0, lax.axis_size("ctx") - 1, retreat, zero_state)
    carried_grads = core_pull((jnp.zeros_like(outputs), arriving))
    feature_grads = tuple((direct_grads[member] + carried_grads[member] for member in range(3)))
    extended_grad, weight_grad = feature_pull(feature_grads)
    spill_rows = extended_grad[:, : KW - 1, :]
    returned = from_behind(spill_rows, "ctx", -1)
    raw_grad = extended_grad[:, KW - 1 :, :]
    raw_grad = raw_grad.at[:, length - (KW - 1) :, :].add(returned)
    rounded = raw_grad.astype(jnp.bfloat16)
    input_grad = lax.psum_scatter(
        jnp.einsum("mtc,mdc->td", rounded, projection, preferred_element_type=jnp.float32),
        "head",
        scatter_dimension=0,
        tiled=True,
    ).astype(jnp.bfloat16)
    kernel_grad = lax.psum(weight_grad, "ctx")
    return (input_grad, kernel_grad)


def solution(mesh):
    return jax.shard_map(
        on_device,
        mesh=mesh,
        in_specs=(
            P("ctx", None),
            P(None, None, "head"),
            P(None, None, "head"),
            P("head", "ctx"),
            P("head", "ctx"),
            P("ctx", "head"),
        ),
        out_specs=(P(("ctx", "head"), None), P(None, None, "head")),
        check_vma=False,
    )
```

profile of v0, /device:TPU:136, one launch (start us, length us, event | category | flops | bytes accessed | tf_op | source)
XLA Modules:
  0.0 1999.5 jit_solution(9301813911177826447)
XLA Ops:
  27.6 80.2 %while.114 = (s32[]{:T(128)}, f32[4,128,128]{2,1,0:T(8,128)S(1)}, f32[3,4,64]{2,0,1:T(4,128)S(1)}, f32[3,4,64,128]{3,2,0,1:T(8,128)}, f32[3,4,64]{2,0,1:T(4,128)...) while((s32[]{:T(128)}, f32[4,128,128]{2,1,0:T(8,128)S(1)}, f32[3,4,64]{2,0,1:T(4,128)S(1)}, ...), condition=%wide.region_3.4_spmd, body=%wide.region_1.0_spmd.sunk | while | flops 151388224 | bytes 2060989 | solution.py:77
  32.0 20.4 %custom-call.38 = f32[4,1,64,64]{2,3,1,0:T(8,128)S(1)} custom-call(f32[4,1,64,64]{3,2,1,0:T(8,128)} %fusion.344), custom_call_target="InvertDiagBlocksLowerTriangular" | custom-call | tf_op jit(solution)/shard_map/while/body/eval_jaxpr/jit(_solve_triangular)/vmap()/triangular_solve | solution.py:50
  58.7 20.4 %custom-call.38 = f32[4,1,64,64]{2,3,1,0:T(8,128)S(1)} custom-call(f32[4,1,64,64]{3,2,1,0:T(8,128)} %fusion.344), custom_call_target="InvertDiagBlocksLowerTriangular" | custom-call | tf_op jit(solution)/shard_map/while/body/eval_jaxpr/jit(_solve_triangular)/vmap()/triangular_solve | solution.py:50
  85.4 20.4 %custom-call.38 = f32[4,1,64,64]{2,3,1,0:T(8,128)S(1)} custom-call(f32[4,1,64,64]{3,2,1,0:T(8,128)} %fusion.344), custom_call_target="InvertDiagBlocksLowerTriangular" | custom-call | tf_op jit(solution)/shard_map/while/body/eval_jaxpr/jit(_solve_triangular)/vmap()/triangular_solve | solution.py:50
  114.6 737.0 %while.115 = (s32[]{:T(128)}, f32[2,128,128]{2,1,0:T(8,128)S(1)}, f32[2,128,128]{2,1,0:T(8,128)}, f32[2,128,128]{2,1,0:T(8,128)}, s32[]{:T(128)}) while((s32[]{:T(128)}, f32[2,128,128]{2,1,0:T(8,128)S(1)}, f32[2,128,128]{2,1,0:T(8,128)}, f32[2,128,128]{2,1,0:T(8,128)}, s32[]{:T(128)}) %tuple.256), condition=%wide.region_5.6_spmd, body=%wide.region_4.5_spmd.sunk | while | flops 50364416 | bytes 1048677 | solution.py:127
  118.4 7.9 collective-permute-done
  130.1 7.9 collective-permute-done
  141.8 7.9 collective-permute-done
  153.5 7.9 collective-permute-done
  165.2 7.9 collective-permute-done
  176.9 7.9 collective-permute-done
  188.6 7.9 collective-permute-done
  200.3 7.9 collective-permute-done
  212.0 7.9 collective-permute-done
  282.2 7.9 collective-permute-done
  305.6 7.9 collective-permute-done
  399.2 7.9 collective-permute-done
  761.9 7.9 collective-permute-done
  851.7 66.0 %while.118 = (s32[]{:T(128)}, f32[2,128,128]{2,1,0:T(8,128)S(1)}, f32[3,2,64,64]{3,2,1,0:T(8,128)}, f32[3,2,64,1]{2,1,3,0:T(2,128)S(1)}, f32[3,2,128,128]{3,2,1,...) while((s32[]{:T(128)}, f32[2,128,128]{2,1,0:T(8,128)S(1)}, ...), condition=%wide.region_9.10_spmd.clone.clone, body=%wide.region_7.9_spmd.clone.clone.sunk | while | flops 88346816 | bytes 2166041 | solution.py:77
  856.4 11.2 custom-call.40
  878.3 11.2 custom-call.40
  900.3 11.2 custom-call.40
  919.8 62.7 %while.119 = (s32[]{:T(128)}, f32[2,128,128]{2,1,0:T(8,128)S(1)}, f32[3,2,64,128]{3,2,0,1:T(8,128)}, f32[3,2,64,128]{3,2,0,1:T(8,128)}, f32[3,2,64,128]{3,2,0,1:...) while((s32[]{:T(128)}, f32[2,128,128]{2,1,0:T(8,128)S(1)}, ...), condition=%wide.region_11.13_spmd.clone, body=%wide.region_10.12_spmd.clone.sunk | while | flops 258445376 | bytes 4060456 | solution.py:77
  923.0 9.8 custom-call.41
  943.9 9.8 custom-call.41
  964.8 9.8 custom-call.41
  982.5 674.3 %while.116 = (s32[]{:T(128)}, f32[2,128,128]{2,1,0:T(8,128)S(1)}, f32[2,128,128]{2,1,0:T(8,128)}, f32[2,128,128]{2,1,0:T(8,128)S(1)}, s32[]{:T(128)}) while((s32[]{:T(128)}, f32[2,128,128]{2,1,0:T(8,128)S(1)}, f32[2,128,128]{2,1,0:T(8,128)}, f32[2,128,128]{2,1,0:T(8,128)S(1)}, s32[]{:T(128)}) %tuple.265), condition=%wide.region_13.15_spmd, body=%wide.region_12.14_spmd.sunk | while | flops 50364416 | bytes 1048677 | solution.py:141
  1658.9 62.7 %while.117 = (s32[]{:T(128)}, f32[2,128,128]{2,1,0:T(8,128)S(1)}, f32[3,2,64,128]{3,2,0,1:T(8,128)}, f32[3,2,64,128]{3,2,0,1:T(8,128)}, f32[3,2,64,128]{3,2,0,1:...) while((s32[]{:T(128)}, f32[2,128,128]{2,1,0:T(8,128)S(1)}, ...), condition=%wide.region_15.17_spmd.clone, body=%wide.region_14.16_spmd.clone.sunk | while | flops 258314432 | bytes 3794713 | solution.py:77
  1662.1 9.8 custom-call.39
  1683.1 9.8 custom-call.39
  1704.0 9.8 custom-call.39
  1739.2 251.2 %psum.7 = f32[3,4,256]{2,0,1:T(4,128)S(1)} all-reduce(f32[3,4,256]{2,0,1:T(4,128)S(1)} %pad_add_fusion.1), channel_id=1, replica_groups=mesh['ctx'=64,'head'=4] {'ctx'}, use_global_device_ids=true, to_apply=%region_23.25 | all-reduce | flops 3072 | bytes 24576 | tf_op jit(solution)/shard_map/psum | solution.py:156
  (726 shorter events, 1474.2 us)
Async XLA Ops:
  7.2 1983.8 %reduce-scatter.2.cloned.1.call-start = ((), (), s32[]{:S(2)}) async-start(), calls=%async_computation.1 | async-start | bytes 1966080 | tf_op jit(solution)/shard_map/reduce_scatter | solution.py:150
  116.5 9.8 collective-permute-start
  128.2 9.8 collective-permute-start
  139.9 9.8 collective-permute-start
  163.3 9.8 collective-permute-start
  175.0 9.8 collective-permute-start
  186.7 9.8 collective-permute-start
  198.4 9.8 collective-permute-start
  210.1 9.8 collective-permute-start
  221.8 9.8 collective-permute-start
  233.5 9.8 collective-permute-start
  256.9 9.8 collective-permute-start
  280.3 9.8 collective-permute-start
  292.0 9.8 collective-permute-start
  303.7 9.8 collective-permute-start
  315.4 9.8 collective-permute-start
  327.1 9.8 collective-permute-start
  350.5 9.8 collective-permute-start
  385.6 9.8 collective-permute-start
  397.3 9.8 collective-permute-start
  409.0 9.8 collective-permute-start
  420.7 9.8 collective-permute-start
  432.4 9.8 collective-permute-start
  444.1 9.8 collective-permute-start
  479.2 9.8 collective-permute-start
  502.6 9.8 collective-permute-start
  514.3 9.8 collective-permute-start
  526.0 9.8 collective-permute-start
  537.7 9.8 collective-permute-start
  549.4 9.8 collective-permute-start
  572.8 9.8 collective-permute-start
  596.2 9.8 collective-permute-start
  (121 other events, 3444.6 us)
Sparse Core Ops, SparseCore 0:
  1739.3 28.3 reduce-scatter.1
where the time goes:
time: 2010 us; the launch traced here: 2000 us
  waiting for transfers between devices  659 us (33%)
  starting transfers between devices  571 us (28%)
  matrix products  287 us (14%)
  blocking collectives  251 us (12%)
  other arithmetic  181 us (9%)
  local copies, waits for them, and re-layouts  32.3 us (2%)
    ppermute x128, waiting for transfers between devices, from_behind(): return lax.ppermute(block, axis, route)  659 us
    ppermute x128, starting transfers between devices, from_behind(): return lax.ppermute(block, axis, route)  571 us
    psum x1, blocking collectives, on_device(): kernel_grad = lax.psum(weight_grad, 'ctx')  251 us
    dot_general x126, matrix products, chain_product(): jnp.einsum('hij,hjk->hik', left_side, right_side, precision=HIGHEST_PRECI...  193 us
    another operation x45, other arithmetic, block_step(): jax.scipy.linalg.solve_triangular(lower_part, target, lower=True, unit_di...  162 us
  transfers between devices with their start and end apart: 129, of which 128 were waited for; matrix products, arithmetic and copies ran while one was open for 0% of the time, Pallas kernels for 0%

commit v1 on v0

--- a/solution.py
+++ b/solution.py
@@ -153,7 +153,7 @@
         scatter_dimension=0,
         tiled=True,
     ).astype(jnp.bfloat16)
-    kernel_grad = lax.psum(weight_grad, "ctx")
+    kernel_grad = jnp.sum(lax.all_gather(weight_grad, "ctx"), 0)
     return (input_grad, kernel_grad)
 
 

time: 2010 us -> 1810 us (0.900)
  blocking collectives: 251 us -> 50.1 us
    psum x1 -> x0, blocking collectives: 251 us -> none  [on_device(): kernel_grad = lax.psum(weight_grad, 'ctx')]
    all_gather x0 -> x1, blocking collectives: none -> 50.1 us  [on_device(): kernel_grad = jnp.sum(lax.all_gather(weight_grad, 'ctx'), 0)]
where the time goes in v1:
time: 1810 us; the launch traced here: 1800 us
  waiting for transfers between devices  659 us (36%)
  starting transfers between devices  571 us (32%)
  matrix products  287 us (16%)
  other arithmetic  181 us (10%)
  blocking collectives  50.1 us (3%)
  local copies, waits for them, and re-layouts  31.7 us (2%)
    ppermute x128, waiting for transfers between devices, from_behind(): return lax.ppermute(block, axis, route)  659 us
    ppermute x128, starting transfers between devices, from_behind(): return lax.ppermute(block, axis, route)  571 us
    dot_general x126, matrix products, chain_product(): jnp.einsum('hij,hjk->hik', left_side, right_side, precision=HIGHEST_PRECI...  193 us
    another operation x45, other arithmetic, block_step(): jax.scipy.linalg.solve_triangular(lower_part, target, lower=True, unit_di...  162 us
    all_gather x1, blocking collectives, on_device(): kernel_grad = jnp.sum(lax.all_gather(weight_grad, 'ctx'), 0)  50.1 us
  transfers between devices with their start and end apart: 129, of which 128 were waited for; matrix products, arithmetic and copies ran while one was open for 0% of the time, Pallas kernels for 0%

profile of v1, /device:TPU:136, one launch (start us, length us, event | category | flops | bytes accessed | tf_op | source)
XLA Modules:
  0.0 1798.7 jit_solution(17508646686910683585)
XLA Ops:
  27.6 80.2 %while.114 = (s32[]{:T(128)}, f32[4,128,128]{2,1,0:T(8,128)S(1)}, f32[3,4,64]{2,0,1:T(4,128)S(1)}, f32[3,4,64,128]{3,2,0,1:T(8,128)}, f32[3,4,64]{2,0,1:T(4,128)...) while((s32[]{:T(128)}, f32[4,128,128]{2,1,0:T(8,128)S(1)}, f32[3,4,64]{2,0,1:T(4,128)S(1)}, ...), condition=%wide.region_3.4_spmd, body=%wide.region_1.0_spmd.sunk | while | flops 151388224 | bytes 2060989 | solution.py:77
  32.0 20.4 %custom-call.38 = f32[4,1,64,64]{2,3,1,0:T(8,128)S(1)} custom-call(f32[4,1,64,64]{3,2,1,0:T(8,128)} %fusion.344), custom_call_target="InvertDiagBlocksLowerTriangular" | custom-call | tf_op jit(solution)/shard_map/while/body/eval_jaxpr/jit(_solve_triangular)/vmap()/triangular_solve | solution.py:50
  58.7 20.4 %custom-call.38 = f32[4,1,64,64]{2,3,1,0:T(8,128)S(1)} custom-call(f32[4,1,64,64]{3,2,1,0:T(8,128)} %fusion.344), custom_call_target="InvertDiagBlocksLowerTriangular" | custom-call | tf_op jit(solution)/shard_map/while/body/eval_jaxpr/jit(_solve_triangular)/vmap()/triangular_solve | solution.py:50
  85.4 20.4 %custom-call.38 = f32[4,1,64,64]{2,3,1,0:T(8,128)S(1)} custom-call(f32[4,1,64,64]{3,2,1,0:T(8,128)} %fusion.344), custom_call_target="InvertDiagBlocksLowerTriangular" | custom-call | tf_op jit(solution)/shard_map/while/body/eval_jaxpr/jit(_solve_triangular)/vmap()/triangular_solve | solution.py:50
  114.6 737.0 %while.115 = (s32[]{:T(128)}, f32[2,128,128]{2,1,0:T(8,128)S(1)}, f32[2,128,128]{2,1,0:T(8,128)}, f32[2,128,128]{2,1,0:T(8,128)}, s32[]{:T(128)}) while((s32[]{:T(128)}, f32[2,128,128]{2,1,0:T(8,128)S(1)}, f32[2,128,128]{2,1,0:T(8,128)}, f32[2,128,128]{2,1,0:T(8,128)}, s32[]{:T(128)}) %tuple.259), condition=%wide.region_5.6_spmd, body=%wide.region_4.5_spmd.sunk | while | flops 50364416 | bytes 1048677 | solution.py:127
  118.4 7.9 collective-permute-done
  130.1 7.9 collective-permute-done
  141.8 7.9 collective-permute-done
  153.5 7.9 collective-permute-done
  165.2 7.9 collective-permute-done
  176.9 7.9 collective-permute-done
  188.6 7.9 collective-permute-done
  200.3 7.9 collective-permute-done
  212.0 7.9 collective-permute-done
  282.2 7.9 collective-permute-done
  305.6 7.9 collective-permute-done
  399.2 7.9 collective-permute-done
  761.9 7.9 collective-permute-done
  851.7 66.0 %while.118 = (s32[]{:T(128)}, f32[2,128,128]{2,1,0:T(8,128)S(1)}, f32[3,2,64,64]{3,2,1,0:T(8,128)}, f32[3,2,64,1]{2,1,3,0:T(2,128)S(1)}, f32[3,2,128,128]{3,2,1,...) while((s32[]{:T(128)}, f32[2,128,128]{2,1,0:T(8,128)S(1)}, ...), condition=%wide.region_9.10_spmd.clone.clone, body=%wide.region_7.9_spmd.clone.clone.sunk | while | flops 88346816 | bytes 2166041 | solution.py:77
  856.4 11.2 custom-call.40
  878.3 11.2 custom-call.40
  900.3 11.2 custom-call.40
  919.8 62.7 %while.119 = (s32[]{:T(128)}, f32[2,128,128]{2,1,0:T(8,128)S(1)}, f32[3,2,64,128]{3,2,0,1:T(8,128)}, f32[3,2,64,128]{3,2,0,1:T(8,128)}, f32[3,2,64,128]{3,2,0,1:...) while((s32[]{:T(128)}, f32[2,128,128]{2,1,0:T(8,128)S(1)}, ...), condition=%wide.region_11.13_spmd.clone, body=%wide.region_10.12_spmd.clone.sunk | while | flops 258445376 | bytes 4060456 | solution.py:77
  923.0 9.8 custom-call.41
  943.9 9.8 custom-call.41
  964.8 9.8 custom-call.41
  982.5 674.3 %while.116 = (s32[]{:T(128)}, f32[2,128,128]{2,1,0:T(8,128)S(1)}, f32[2,128,128]{2,1,0:T(8,128)}, f32[2,128,128]{2,1,0:T(8,128)S(1)}, s32[]{:T(128)}) while((s32[]{:T(128)}, f32[2,128,128]{2,1,0:T(8,128)S(1)}, f32[2,128,128]{2,1,0:T(8,128)}, f32[2,128,128]{2,1,0:T(8,128)S(1)}, s32[]{:T(128)}) %tuple.268), condition=%wide.region_13.15_spmd, body=%wide.region_12.14_spmd.sunk | while | flops 50364416 | bytes 1048677 | solution.py:141
  1658.9 62.7 %while.117 = (s32[]{:T(128)}, f32[2,128,128]{2,1,0:T(8,128)S(1)}, f32[3,2,64,128]{3,2,0,1:T(8,128)}, f32[3,2,64,128]{3,2,0,1:T(8,128)}, f32[3,2,64,128]{3,2,0,1:...) while((s32[]{:T(128)}, f32[2,128,128]{2,1,0:T(8,128)S(1)}, ...), condition=%wide.region_15.17_spmd.clone, body=%wide.region_14.16_spmd.clone.sunk | while | flops 258314432 | bytes 3794713 | solution.py:77
  1662.1 9.8 custom-call.39
  1683.1 9.8 custom-call.39
  1704.0 9.8 custom-call.39
  1739.3 50.1 %all-gather = f32[192,4,256]{2,1,0:T(4,128)S(1)} all-gather(f32[3,4,256]{2,1,0:T(4,128)S(1)} %pad_add_fusion.2), channel_id=2, replica_groups=mesh['ctx'=64,'head'=4] {'ctx'}, dimensions={0}, use_global_device_ids=true | all-gather | bytes 798720 | tf_op jit(solution)/shard_map/all_gather | solution.py:156
  (730 shorter events, 1474.3 us)
Async XLA Ops:
  7.2 1782.9 %reduce-scatter.2.cloned.1.call-start = ((), (), s32[]{:S(2)}) async-start(), calls=%async_computation.1 | async-start | bytes 1966080 | tf_op jit(solution)/shard_map/reduce_scatter | solution.py:150
  116.5 9.8 collective-permute-start
  128.2 9.8 collective-permute-start
  139.9 9.8 collective-permute-start
  151.6 9.8 collective-permute-start
  175.0 9.8 collective-permute-start
  186.7 9.8 collective-permute-start
  198.4 9.8 collective-permute-start
  210.1 9.8 collective-permute-start
  221.8 9.8 collective-permute-start
  233.5 9.8 collective-permute-start
  256.9 9.8 collective-permute-start
  280.3 9.8 collective-permute-start
  292.0 9.8 collective-permute-start
  303.7 9.8 collective-permute-start
  315.4 9.8 collective-permute-start
  327.1 9.8 collective-permute-start
  350.5 9.8 collective-permute-start
  385.6 9.8 collective-permute-start
  397.3 9.8 collective-permute-start
  409.0 9.8 collective-permute-start
  420.7 9.8 collective-permute-start
  432.4 9.8 collective-permute-start
  444.1 9.8 collective-permute-start
  479.2 9.8 collective-permute-start
  502.6 9.8 collective-permute-start
  514.3 9.8 collective-permute-start
  526.0 9.8 collective-permute-start
  537.7 9.8 collective-permute-start
  549.4 9.8 collective-permute-start
  572.8 9.8 collective-permute-start
  596.2 9.8 collective-permute-start
  (121 other events, 3444.6 us)
Sparse Core Ops, SparseCore 0:
  1739.3 28.4 reduce-scatter.1
